TPU v7x, 32 devices: a whole 2x2x4 slice. The times are simulated.
32 devices in a mesh: fsdp: 16 (over z, y, x), dp: 2 (over core).
Axes of the slice: x: 2, y: 2, z: 4, core: 2. Of those that a mesh axis runs over, the one named last changes fastest.
Arguments:
- grads: bfloat16 [2, 1024, 28672], P('dp', 'fsdp')
- block_slot: int32 [28], replicated, may hold values from 0 to 31, as said below
- left_stats: float32 [32, 1024, 1024], P('fsdp', 'dp')
- right_stats: float32 [32, 1024, 1024], P('fsdp', 'dp')
- left_root: bfloat16 [32, 1024, 1024], P('fsdp', 'dp')
- right_root: bfloat16 [32, 1024, 1024], P('fsdp', 'dp')
Outputs:
- left_new: float32 [32, 1024, 1024], P('fsdp', 'dp')
- right_new: float32 [32, 1024, 1024], P('fsdp', 'dp')
- update: bfloat16 [1024, 28672], P('fsdp')
Inputs may be any that keep to these rules, and one draw needn't show every extreme that they name: The entries of block_slot are distinct. Block b's statistics and roots sit in slot block_slot[b], which belongs to the fsdp device of index block_slot[b] // 2; slots that no block names are empty and their statistics pass through unchanged.
All inputs are finite; a program needn't handle non-finite values.
Results may differ from a plain program's by a relative error of at most 0.015.
Values may be sent and summed in bfloat16 or wider, within the bound.
A program may use at most 128 MiB of HBM per device.

v0:
```python
import jax
import jax.numpy as jnp
from jax import lax
from jax.sharding import PartitionSpec as P

epsilon = 1e-06


def per_device(grads, block_slot, left_stats, right_stats, left_root, right_root):
    local_rows = grads[0]
    row_dev, col_count = local_rows.shape
    block_size = left_stats.shape[2]
    block_count = col_count // block_size
    slot_count = left_stats.shape[0]
    shared_rows = left_stats.shape[1]
    total_slots = slot_count * lax.axis_size("fsdp")
    slot_ids = jnp.arange(total_slots, dtype=jnp.int32)
    matches = block_slot[None, :] == slot_ids[:, None]
    filled = jnp.any(matches, axis=1)
    source = jnp.sum(
        jnp.where(matches, jnp.arange(block_count, dtype=jnp.int32)[None, :], 0), axis=1
    )
    row_start = lax.axis_index("dp") * shared_rows
    band = local_rows.astype(jnp.float32).reshape(row_dev, block_count, block_size)
    shares = lax.psum_scatter(band.astype(jnp.bfloat16), "dp", scatter_dimension=2, tiled=True)
    outgoing = jnp.where(
        filled[None, :, None], jnp.take(shares, source, axis=1), jnp.zeros((), jnp.bfloat16)
    )
    incoming = lax.all_to_all(outgoing, "fsdp", split_axis=1, concat_axis=0, tiled=True)
    gradient = lax.all_gather(incoming, "dp", axis=2, tiled=True)
    own_rows = lax.dynamic_slice_in_dim(gradient, row_start, shared_rows, 0)
    whole_right = lax.all_gather(right_root, "dp", axis=1, tiled=True)
    left_new = left_stats + jnp.einsum(
        "rjc,kjc->jrk", own_rows, gradient, preferred_element_type=jnp.float32
    )
    columns = lax.dynamic_slice_in_dim(gradient, row_start, shared_rows, 2)
    right_new = right_stats + jnp.einsum(
        "rjc,rjk->jck", columns, gradient, preferred_element_type=jnp.float32
    )
    left_applied = jnp.einsum(
        "jrk,kjc->rjc", left_root, gradient, preferred_element_type=jnp.float32
    ).astype(jnp.bfloat16)
    both_applied = jnp.einsum(
        "rjc,jck->rjk", left_applied, whole_right, preferred_element_type=jnp.float32
    )
    squares = lax.psum(jnp.sum(both_applied * both_applied, axis=(0, 2)), "dp")
    factor = lax.rsqrt(squares / (block_size * block_size) + epsilon)
    scaled = (both_applied * factor[None, :, None]).astype(jnp.bfloat16)
    full_rows = lax.all_gather(scaled, "dp", axis=0, tiled=True)
    returned = lax.all_to_all(full_rows, "fsdp", split_axis=0, concat_axis=1, tiled=True)
    update = jnp.take(returned, block_slot, axis=1).reshape(row_dev, col_count)
    return (left_new, right_new, update)


def solution(mesh):
    in_specs = (
        P("dp", "fsdp", None),
        P(),
        P("fsdp", "dp", None),
        P("fsdp", "dp", None),
        P("fsdp", "dp", None),
        P("fsdp", "dp", None),
    )
    out_specs = (P("fsdp", "dp", None), P("fsdp", "dp", None), P("fsdp", None))
    return jax.shard_map(
        per_device, mesh=mesh, in_specs=in_specs, out_specs=out_specs, check_vma=False
    )
```

profile of v0, /device:TPU:14, one launch (start us, length us, event | category | flops | bytes accessed | tf_op | source)
XLA Modules:
  0.0 272.9 jit_solution(7911280126792472011)
XLA Ops:
  7.2 5.7 %squeeze.3 = bf16[64,28,1024]{2,1,0:T(8,128)(2,1)} reshape(bf16[1,64,28672]{2,1,0:T(8,128)(2,1)} %param.6) | data formatting | bytes 7340032 | tf_op jit(solution)/shard_map/squeeze | solution.py:10
  12.9 6.0 %copy.31 = bf16[64,28,1024]{2,0,1:T(8,128)(2,1)} copy(bf16[64,28,1024]{2,1,0:T(8,128)(2,1)} %squeeze.3) | data formatting | bytes 7340032 | tf_op jit(solution)/shard_map/squeeze | solution.py:10
  19.0 0.7 all-gather.6.cloned.1.call-update
  19.9 0.1 fusion.16
  20.1 12.2 %reduce-scatter.2.cloned.1.call-done = bf16[64,28,512]{2,0,1:T(8,128)(2,1)} async-done(((bf16[64,28,1024]{2,0,1:T(8,128)(2,1)}), bf16[64,28,512]{2,0,1:T(8,128)(2,1)}) %reduce-scatter.2.cloned.1.call-update) | async-done | bytes 1835024 | tf_op jit(solution)/shard_map/reduce_scatter | solution.py:25
  32.3 3.5 %gather_fusion = bf16[32,64,512]{2,1,0:T(8,128)(2,1)} fusion(bf16[64,28,512]{2,0,1:T(8,128)(2,1)} %reduce-scatter.2.cloned.1.call-done, s32[1024]{0:T(1024)S(1)} %pad_clamp_fusion.1), kind=kCustom, calls=%fused_computation | custom fusion | bytes 4194432 | tf_op jit(solution)/shard_map/jit(_take)/gather | solution.py:27
  35.8 1.9 select_bitcast_fusion
  37.7 53.8 %all_to_all.36 = bf16[64,32,512]{2,0,1:T(8,128)(2,1)S(1)} all-to-all(bf16[64,32,512]{2,0,1:T(8,128)(2,1)S(1)} %select_bitcast_fusion), channel_id=1, replica_groups=mesh['fsdp'=16,'dp'=2] {'fsdp'}, dimensions={1} | all-to-all | bytes 4194304 | tf_op jit(solution)/shard_map/all_to_all | solution.py:29
  91.5 1.5 copy.32
  93.1 14.0 %all-gather.4.cloned.1.call-done = bf16[1024,2,1024]{2,0,1:T(8,128)(2,1)} async-done(((bf16[1024,2,512]{2,0,1:T(8,128)(2,1)}), bf16[1024,2,1024]{2,0,1:T(8,128)(2,1)}) %all-gather.4.cloned.1.call-update) | async-done | bytes 4194320 | tf_op jit(solution)/shard_map/all_gather | solution.py:30
  107.0 10.4 %multiply_reduce_fusion = (f32[2]{0:T(128)S(1)}, f32[2,512,1024]{2,1,0:T(8,128)}) fusion(bf16[2,1024,1024]{2,1,0:T(8,128)(2,1)} %all-gather.6.cloned.1.call-done, bf16[1024,2,1024]{2,0,1:T(8,128)(2,1)} %all-gather.4.cloned.1.call-done, bf16[2,512,1024]{2,1,0:T(8,128)(2,1)S(1)} %copy-done), kind=kOutput, calls=%fused_computation.3 | convolution fusion | flops 4298113024 | bytes 14680072 | tf_op jit(solution)/shard_map/rjc,jck->rjk/dot_general | solution.py:43
  117.5 2.6 psum.7
  120.1 4.1 %fusion = bf16[512,2,1024]{2,0,1:T(8,128)(2,1)} fusion(f32[2,512,1024]{2,1,0:T(8,128)} %get-tuple-element.4, f32[2]{0:T(128)S(1)} %add_rsqrt_fusion), kind=kLoop, calls=%fused_computation.5 | loop fusion | flops 2097152 | bytes 6291464 | tf_op jit(solution)/shard_map/convert_element_type | solution.py:48
  124.3 15.0 %all-gather.8.cloned.1.call-done = bf16[1024,2,1024]{2,0,1:T(8,128)(2,1)} async-done(((bf16[512,2,1024]{2,0,1:T(8,128)(2,1)}), bf16[1024,2,1024]{2,0,1:T(8,128)(2,1)}) %all-gather.8.cloned.1.call-update) | async-done | bytes 4194320 | tf_op jit(solution)/shard_map/all_gather | solution.py:49
  139.3 8.5 %copy.36 = bf16[1024,2,1024]{2,1,0:T(2,128)(2,1)} copy(bf16[1024,2,1024]{2,0,1:T(8,128)(2,1)} %all-gather.8.cloned.1.call-done) | data formatting | bytes 8388608 | tf_op jit(solution)/shard_map/all_gather | solution.py:49
  147.7 7.0 %all-to-all-start.1 = ((bf16[1024,2,1024]{2,1,0:T(2,128)(2,1)}), bf16[1024,2,1024]{2,1,0:T(2,128)(2,1)}, u32[]{:S(2)}, u32[]{:S(2)}) async-start(bf16[1024,2,1024]{2,1,0:T(2,128)(2,1)} %copy.36), calls=%async_computation.2 | async-start | bytes 8388608 | tf_op jit(solution)/shard_map/all_to_all | solution.py:50
  154.9 8.6 %fusion.8 = f32[2,512,1024]{2,1,0:T(8,128)} fusion(f32[2,512,1024]{2,1,0:T(8,128)} %param.8, bf16[1024,2,1024]{2,0,1:T(8,128)(2,1)} %all-gather.4.cloned.1.call-done, s32[]{:T(128)S(6)} %select_n.47), kind=kOutput, calls=%fused_computation.14 | convolution fusion | flops 2148532224 | bytes 14680068 | tf_op jit(solution)/shard_map/rjc,kjc->jrk/dot_general | solution.py:33
  163.5 4.5 %fusion.11 = f32[2,512,1024]{2,1,0:T(8,128)} fusion(f32[2,512,1024]{2,1,0:T(8,128)S(1)} %copy-done.2, bf16[1024,2,1024]{2,0,1:T(8,128)(2,1)S(1)} %copy-done.3, s32[]{:T(128)S(6)} %select_n.47), kind=kOutput, calls=%fused_computation.15 | convolution fusion | flops 2148532224 | bytes 14680068 | tf_op jit(solution)/shard_map/rjc,rjk->jck/dot_general | solution.py:37
  167.9 82.6 %all-to-all-done.1 = bf16[1024,2,1024]{2,1,0:T(2,128)(2,1)} async-done(((bf16[1024,2,1024]{2,1,0:T(2,128)(2,1)}), bf16[1024,2,1024]{2,1,0:T(2,128)(2,1)}, u32[]{:S(2)}, u32[]{:S(2)}) %all-to-all-start.1) | async-done | bytes 4194336 | tf_op jit(solution)/shard_map/all_to_all | solution.py:50
  250.5 3.5 %copy.37 = bf16[1024,2,1024]{2,0,1:T(8,128)(2,1)S(1)} copy(bf16[1024,2,1024]{2,1,0:T(2,128)(2,1)} %all-to-all-done.1) | data formatting | bytes 8388608 | tf_op jit(solution)/shard_map/all_to_all | solution.py:50
  254.0 2.4 copy.38
  256.4 4.9 %gather_fusion.1 = bf16[28,64,1024]{2,1,0:T(8,128)(2,1)} fusion(bf16[64,32,1024]{2,0,1:T(8,128)(2,1)} %bitcast.30, s32[1024]{0:T(1024)S(1)} %pad_clamp_fusion), kind=kCustom, calls=%fused_computation.1 | custom fusion | bytes 7340144 | tf_op jit(solution)/shard_map/jit(_take)/gather | solution.py:51
  261.2 2.6 copy.43
  263.8 2.6 broadcast_select_fusion
  (28 shorter events, 0.5 us)
Async XLA Ops:
  7.2 99.9 %copy-start = (bf16[2,512,1024]{2,1,0:T(8,128)(2,1)S(1)}, bf16[2,512,1024]{2,1,0:T(8,128)(2,1)}, u32[]{:S(2)}) copy-start(bf16[2,512,1024]{2,1,0:T(8,128)(2,1)} %param.10) | copy-start | bytes 6291460
  7.2 25.1 %reduce-scatter.2.cloned.1.call-start = ((), (), s32[]{:S(2)}) async-start(), calls=%async_computation.3 | async-start | bytes 5505024 | tf_op jit(solution)/shard_map/reduce_scatter | solution.py:25
  19.0 0.8 copy-start.4
  19.0 74.0 %all-gather.6.cloned.1.call-start = ((), (), s32[]{:S(2)}) async-start(), calls=%async_computation.5 | async-start | bytes 6291456 | tf_op jit(solution)/shard_map/all_gather | solution.py:32
  19.8 87.3 %all-gather.4.cloned.1.call-start = ((), (), s32[]{:S(2)}) async-start(), calls=%async_computation.4 | async-start | bytes 6291456 | tf_op jit(solution)/shard_map/all_gather | solution.py:30
  93.0 46.3 %all-gather.8.cloned.1.call-start = ((), (), s32[]{:S(2)}) async-start(), calls=%async_computation.6 | async-start | bytes 6291456 | tf_op jit(solution)/shard_map/all_gather | solution.py:49
  147.7 102.8 %all-to-all-start.1 = ((bf16[1024,2,1024]{2,1,0:T(2,128)(2,1)}), bf16[1024,2,1024]{2,1,0:T(2,128)(2,1)}, u32[]{:S(2)}, u32[]{:S(2)}) async-start(bf16[1024,2,1024]{2,1,0:T(2,128)(2,1)} %copy.36), calls=%async_computation.2 | async-start | bytes 8388608 | tf_op jit(solution)/shard_map/all_to_all | solution.py:50
  154.9 8.6 %copy-start.2 = (f32[2,512,1024]{2,1,0:T(8,128)S(1)}, f32[2,512,1024]{2,1,0:T(8,128)}, u32[]{:S(2)}) copy-start(f32[2,512,1024]{2,1,0:T(8,128)} %param.9) | copy-start | bytes 12582916
  154.9 8.6 %copy-start.3 = (bf16[1024,2,1024]{2,0,1:T(8,128)(2,1)S(1)}, bf16[1024,2,1024]{2,0,1:T(8,128)(2,1)}, u32[]{:S(2)}) copy-start(bf16[1024,2,1024]{2,0,1:T(8,128)(2,1)} %all-gather.4.cloned.1.call-done) | copy-start | bytes 12582916
  261.2 5.1 %copy-start.1 = (bf16[2,512,1024]{2,1,0:T(8,128)(2,1)S(1)}, bf16[2,512,1024]{2,1,0:T(8,128)(2,1)}, u32[]{:S(2)}) copy-start(bf16[2,512,1024]{2,1,0:T(8,128)(2,1)} %param.10) | copy-start | bytes 6291460
Sparse Core Ops, SparseCore 0:
  19.1 13.0 reduce-scatter.1
  33.8 14.8 all-gather.5
  93.1 13.8 all-gather.3
  124.4 14.8 all-gather.7
where the time goes:
time: 273 us
  waiting for transfers between devices  124 us (45%)
  blocking collectives  56.4 us (21%)
  local copies, waits for them, and re-layouts  38.6 us (14%)
  matrix products  23.5 us (9%)
  between operations  13.9 us (5%)
  other arithmetic  8.9 us (3%)
  starting transfers between devices  7.12 us (3%)
    all_to_all x1, waiting for transfers between devices, per_device(): lax.all_to_all(full_rows, 'fsdp', split_axis=0, concat_axis=1, tiled=True)  82.6 us
    all_to_all x1, blocking collectives, per_device(): lax.all_to_all(outgoing, 'fsdp', split_axis=1, concat_axis=0, tiled=True)  53.8 us
    all_gather x1, waiting for transfers between devices, per_device(): full_rows = lax.all_gather(scaled, 'dp', axis=0, tiled=True)  15 us
    all_gather x1, waiting for transfers between devices, per_device(): gradient = lax.all_gather(incoming, 'dp', axis=2, tiled=True)  14 us
    reduce_scatter x1, waiting for transfers between devices, per_device(): lax.psum_scatter(band.astype(jnp.bfloat16), 'dp', scatter_dimension=2, ti...  12.2 us
    squeeze x2, local copies, waits for them, and re-layouts, per_device(): local_rows = grads[0]  11.7 us
    dot_general x1, matrix products, per_device(): jnp.einsum('rjc,jck->rjk', left_applied, whole_right, preferred_element_t...  10.4 us
    dot_general x1, matrix products, per_device(): jnp.einsum('rjc,kjc->jrk', own_rows, gradient, preferred_element_type=jnp...  8.58 us
  transfers between devices with their start and end apart: 5, of which 4 were waited for; matrix products, arithmetic and copies ran while one was open for 7% of the time, Pallas kernels for 0%

commit v1 on v0

--- a/solution.py
+++ b/solution.py
@@ -47,7 +47,9 @@
     factor = lax.rsqrt(squares / (block_size * block_size) + epsilon)
     scaled = (both_applied * factor[None, :, None]).astype(jnp.bfloat16)
     full_rows = lax.all_gather(scaled, "dp", axis=0, tiled=True)
-    returned = lax.all_to_all(full_rows, "fsdp", split_axis=0, concat_axis=1, tiled=True)
+    parts = jnp.split(full_rows, lax.axis_size("fsdp"), axis=0)
+    received = lax.all_to_all(jnp.stack(parts), "fsdp", 0, 0)
+    returned = jnp.concatenate(received, axis=1)
     update = jnp.take(returned, block_slot, axis=1).reshape(row_dev, col_count)
     return (left_new, right_new, update)
 

time: 273 us -> 286 us (1.048)
  local copies, waits for them, and re-layouts: 38.6 us -> 51.1 us
    unnamed x10 -> x25, local copies, waits for them, and re-layouts: 0.03 us -> 25.1 us
    all_gather x1 -> x0, local copies, waits for them, and re-layouts: 8.48 us -> none  [per_device(): full_rows = lax.all_gather(scaled, 'dp', axis=0, tiled=True)]
    all_to_all x2 -> x0, local copies, waits for them, and re-layouts: 5.86 us -> none  [per_device(): lax.all_to_all(full_rows, 'fsdp', split_axis=0, concat_axis=1, tiled=True)]
    dot_general x1, matrix products: 8.58 us -> 4.4 us  [per_device(): jnp.einsum('rjc,kjc->jrk', own_rows, gradient, preferred_element_type=jnp...]
    dot_general x1, matrix products: 4.46 us -> 8.6 us  [per_device(): jnp.einsum('rjc,rjk->jck', columns, gradient, preferred_element_type=jnp....]
where the time goes in v1:
time: 286 us; the launch traced here: 285 us
  waiting for transfers between devices  125 us (44%)
  blocking collectives  56.2 us (20%)
  local copies, waits for them, and re-layouts  51.1 us (18%)
  matrix products  23.4 us (8%)
  between operations  13.9 us (5%)
  other arithmetic  8.9 us (3%)
  starting transfers between devices  7.12 us (2%)
    all_to_all x1, waiting for transfers between devices, per_device(): received = lax.all_to_all(jnp.stack(parts), 'fsdp', 0, 0)  82.6 us
    all_to_all x1, blocking collectives, per_device(): lax.all_to_all(outgoing, 'fsdp', split_axis=1, concat_axis=0, tiled=True)  53.8 us
    unnamed x25, local copies, waits for them, and re-layouts  25.1 us
    all_gather x1, waiting for transfers between devices, per_device(): full_rows = lax.all_gather(scaled, 'dp', axis=0, tiled=True)  15 us
    all_gather x1, waiting for transfers between devices, per_device(): gradient = lax.all_gather(incoming, 'dp', axis=2, tiled=True)  14 us
    reduce_scatter x1, waiting for transfers between devices, per_device(): lax.psum_scatter(band.astype(jnp.bfloat16), 'dp', scatter_dimension=2, ti...  12.2 us
    squeeze x2, local copies, waits for them, and re-layouts, per_device(): local_rows = grads[0]  11.7 us
    dot_general x1, matrix products, per_device(): jnp.einsum('rjc,jck->rjk', left_applied, whole_right, preferred_element_t...  10.4 us
  transfers between devices with their start and end apart: 5, of which 4 were waited for; matrix products, arithmetic and copies ran while one was open for 7% of the time, Pallas kernels for 0%

profile of v1, /device:TPU:14, one launch (start us, length us, event | category | flops | bytes accessed | tf_op | source)
XLA Modules:
  0.0 285.2 jit_solution(7871406676072884298)
XLA Ops:
  7.2 5.7 %squeeze.3 = bf16[64,28,1024]{2,1,0:T(8,128)(2,1)} reshape(bf16[1,64,28672]{2,1,0:T(8,128)(2,1)} %param.6) | data formatting | bytes 7340032 | tf_op jit(solution)/shard_map/squeeze | solution.py:10
  12.9 6.0 %copy.20 = bf16[64,28,1024]{2,0,1:T(8,128)(2,1)} copy(bf16[64,28,1024]{2,1,0:T(8,128)(2,1)} %squeeze.3) | data formatting | bytes 7340032 | tf_op jit(solution)/shard_map/squeeze | solution.py:10
  20.1 12.2 %reduce-scatter.2.cloned.1.call-done = bf16[64,28,512]{2,0,1:T(8,128)(2,1)} async-done(((bf16[64,28,1024]{2,0,1:T(8,128)(2,1)}), bf16[64,28,512]{2,0,1:T(8,128)(2,1)}) %reduce-scatter.2.cloned.1.call-update) | async-done | bytes 1835024 | tf_op jit(solution)/shard_map/reduce_scatter | solution.py:25
  32.3 3.5 %gather_fusion = bf16[32,64,512]{2,1,0:T(8,128)(2,1)} fusion(bf16[64,28,512]{2,0,1:T(8,128)(2,1)} %reduce-scatter.2.cloned.1.call-done, s32[1024]{0:T(1024)S(1)} %pad_clamp_fusion.1), kind=kCustom, calls=%fused_computation | custom fusion | bytes 4194432 | tf_op jit(solution)/shard_map/jit(_take)/gather | solution.py:27
  35.8 1.9 select_bitcast_fusion
  37.7 53.8 %all_to_all.23 = bf16[64,32,512]{2,0,1:T(8,128)(2,1)S(1)} all-to-all(bf16[64,32,512]{2,0,1:T(8,128)(2,1)S(1)} %select_bitcast_fusion), channel_id=1, replica_groups=mesh['fsdp'=16,'dp'=2] {'fsdp'}, dimensions={1} | all-to-all | bytes 4194304 | tf_op jit(solution)/shard_map/all_to_all | solution.py:29
  93.1 14.0 %all-gather.4.cloned.1.call-done = bf16[1024,2,1024]{2,0,1:T(8,128)(2,1)} async-done(((bf16[1024,2,512]{2,0,1:T(8,128)(2,1)}), bf16[1024,2,1024]{2,0,1:T(8,128)(2,1)}) %all-gather.4.cloned.1.call-update) | async-done | bytes 4194320 | tf_op jit(solution)/shard_map/all_gather | solution.py:30
  107.1 10.4 %multiply_reduce_fusion = (f32[2]{0:T(128)S(1)}, f32[2,512,1024]{2,1,0:T(8,128)}) fusion(bf16[2,1024,1024]{2,1,0:T(8,128)(2,1)} %all-gather.6.cloned.1.call-done, bf16[1024,2,1024]{2,0,1:T(8,128)(2,1)} %all-gather.4.cloned.1.call-done, bf16[2,512,1024]{2,1,0:T(8,128)(2,1)S(1)} %copy-done), kind=kOutput, calls=%fused_computation.3 | convolution fusion | flops 4298113024 | bytes 14680072 | tf_op jit(solution)/shard_map/rjc,jck->rjk/dot_general | solution.py:43
  117.5 2.4 psum.7
  120.0 4.1 %fusion = bf16[512,2,1024]{2,0,1:T(8,128)(2,1)} fusion(f32[2,512,1024]{2,1,0:T(8,128)} %get-tuple-element.4, f32[2]{0:T(128)S(1)} %add_rsqrt_fusion), kind=kLoop, calls=%fused_computation.5 | loop fusion | flops 2097152 | bytes 6291464 | tf_op jit(solution)/shard_map/convert_element_type | solution.py:48
  124.2 15.0 %all-gather.8.cloned.1.call-done = bf16[1024,2,1024]{2,0,1:T(8,128)(2,1)} async-done(((bf16[512,2,1024]{2,0,1:T(8,128)(2,1)}), bf16[1024,2,1024]{2,0,1:T(8,128)(2,1)}) %all-gather.8.cloned.1.call-update) | async-done | bytes 4194320 | tf_op jit(solution)/shard_map/all_gather | solution.py:49
  139.2 1.7 fusion.31
  140.9 1.7 fusion.30
  142.5 1.7 fusion.29
  144.2 1.7 fusion.28
  155.9 1.7 fusion.21
  157.6 1.7 fusion.20
  165.9 7.0 %all-to-all-start.1 = ((bf16[16,64,2,1024]{3,1,2,0:T(8,128)(2,1)}), bf16[16,64,2,1024]{3,1,2,0:T(8,128)(2,1)}, u32[]{:S(2)}, u32[]{:S(2)}) async-start(bf16[16,64,2,1024]{3,1,2,0:T(8,128)(2,1)} %fusion.16), calls=%async_computation.2 | async-start | bytes 8388608 | tf_op jit(solution)/shard_map/all_to_all | solution.py:51
  173.0 8.6 %fusion.11 = f32[2,512,1024]{2,1,0:T(8,128)} fusion(f32[2,512,1024]{2,1,0:T(8,128)} %param.9, bf16[1024,2,1024]{2,0,1:T(8,128)(2,1)} %all-gather.4.cloned.1.call-done, s32[]{:T(128)S(6)} %select_n.47), kind=kOutput, calls=%fused_computation.15 | convolution fusion | flops 2148532224 | bytes 14680068 | tf_op jit(solution)/shard_map/rjc,rjk->jck/dot_general | solution.py:37
  181.6 4.4 %fusion.8 = f32[2,512,1024]{2,1,0:T(8,128)} fusion(f32[2,512,1024]{2,1,0:T(8,128)S(1)} %copy-done.2, bf16[1024,2,1024]{2,0,1:T(8,128)(2,1)S(1)} %copy-done.3, s32[]{:T(128)S(6)} %select_n.47), kind=kOutput, calls=%fused_computation.14 | convolution fusion | flops 2148532224 | bytes 14680068 | tf_op jit(solution)/shard_map/rjc,kjc->jrk/dot_general | solution.py:33
  186.0 82.6 %all-to-all-done.1 = bf16[16,64,2,1024]{3,1,2,0:T(8,128)(2,1)} async-done(((bf16[16,64,2,1024]{3,1,2,0:T(8,128)(2,1)}), bf16[16,64,2,1024]{3,1,2,0:T(8,128)(2,1)}, u32[]{:S(2)}, u32[]{:S(2)}) %all-to-all-start.1) | async-done | bytes 4194336 | tf_op jit(solution)/shard_map/all_to_all | solution.py:51
  268.6 4.9 %gather_fusion.1 = bf16[28,64,1024]{2,1,0:T(8,128)(2,1)} fusion(bf16[64,32,1024]{2,0,1:T(8,128)(2,1)} %bitcast.25, s32[1024]{0:T(1024)S(1)} %pad_clamp_fusion), kind=kCustom, calls=%fused_computation.1 | custom fusion | bytes 7340144 | tf_op jit(solution)/shard_map/jit(_take)/gather | solution.py:53
  273.5 2.6 copy.29
  276.1 2.6 broadcast_select_fusion
  (41 shorter events, 19.5 us)
Async XLA Ops:
  7.2 100.0 %copy-start = (bf16[2,512,1024]{2,1,0:T(8,128)(2,1)S(1)}, bf16[2,512,1024]{2,1,0:T(8,128)(2,1)}, u32[]{:S(2)}) copy-start(bf16[2,512,1024]{2,1,0:T(8,128)(2,1)} %param.10) | copy-start | bytes 6291460
  7.2 25.1 %reduce-scatter.2.cloned.1.call-start = ((), (), s32[]{:S(2)}) async-start(), calls=%async_computation.3 | async-start | bytes 5505024 | tf_op jit(solution)/shard_map/reduce_scatter | solution.py:25
  19.0 0.8 copy-start.4
  19.0 74.1 %all-gather.6.cloned.1.call-start = ((), (), s32[]{:S(2)}) async-start(), calls=%async_computation.5 | async-start | bytes 6291456 | tf_op jit(solution)/shard_map/all_gather | solution.py:32
  19.8 87.4 %all-gather.4.cloned.1.call-start = ((), (), s32[]{:S(2)}) async-start(), calls=%async_computation.4 | async-start | bytes 6291456 | tf_op jit(solution)/shard_map/all_gather | solution.py:30
  93.1 46.1 %all-gather.8.cloned.1.call-start = ((), (), s32[]{:S(2)}) async-start(), calls=%async_computation.6 | async-start | bytes 6291456 | tf_op jit(solution)/shard_map/all_gather | solution.py:49
  165.9 102.8 %all-to-all-start.1 = ((bf16[16,64,2,1024]{3,1,2,0:T(8,128)(2,1)}), bf16[16,64,2,1024]{3,1,2,0:T(8,128)(2,1)}, u32[]{:S(2)}, u32[]{:S(2)}) async-start(bf16[16,64,2,1024]{3,1,2,0:T(8,128)(2,1)} %fusion.16), calls=%async_computation.2 | async-start | bytes 8388608 | tf_op jit(solution)/shard_map/all_to_all | solution.py:51
  173.0 8.6 %copy-start.2 = (f32[2,512,1024]{2,1,0:T(8,128)S(1)}, f32[2,512,1024]{2,1,0:T(8,128)}, u32[]{:S(2)}) copy-start(f32[2,512,1024]{2,1,0:T(8,128)} %param.8) | copy-start | bytes 12582916
  173.0 8.6 %copy-start.3 = (bf16[1024,2,1024]{2,0,1:T(8,128)(2,1)S(1)}, bf16[1024,2,1024]{2,0,1:T(8,128)(2,1)}, u32[]{:S(2)}) copy-start(bf16[1024,2,1024]{2,0,1:T(8,128)(2,1)} %all-gather.4.cloned.1.call-done) | copy-start | bytes 12582916
  273.5 5.1 %copy-start.1 = (bf16[2,512,1024]{2,1,0:T(8,128)(2,1)S(1)}, bf16[2,512,1024]{2,1,0:T(8,128)(2,1)}, u32[]{:S(2)}) copy-start(bf16[2,512,1024]{2,1,0:T(8,128)(2,1)} %param.10) | copy-start | bytes 6291460
Sparse Core Ops, SparseCore 0:
  19.1 13.0 reduce-scatter.1
  33.8 14.8 all-gather.5
  93.2 13.8 all-gather.3
  124.3 14.8 all-gather.7
